TPU v7x, 128 devices: a whole 4x4x4 slice. The times are simulated.
128 devices in a mesh: dp: 16 (over x_lo, z, core), chan: 8 (over y, x_hi).
Axes of the slice: x: 4 (x_hi: 2, x_lo: 2; x = x_hi * 2 + x_lo), y: 4, z: 4, core: 2. Of those that a mesh axis runs over, the one named last changes fastest.
Arguments:
- volume: bfloat16 [16, 512, 1024], P('dp', 'chan'), may hold values from -16 to 16
- w_first: bfloat16 [27, 512, 512], P(None, 'chan'), may hold values from -0.0546875 to 0.0546875
- gain: float32 [512], replicated, may hold values from 0.1 to 1.9
- w_second: bfloat16 [27, 512, 512], P(None, None, 'chan'), may hold values from -0.0546875 to 0.0546875
- cotangent: bfloat16 [16, 512, 1024], P('dp', 'chan'), may hold values from -8 to 8
Outputs:
- output: bfloat16 [16, 512, 1024], P('dp', 'chan')
- grad_volume: bfloat16 [16, 512, 1024], P('dp', 'chan')
- grad_w_first: float32 [27, 512, 512], P(None, 'chan')
- grad_gain: float32 [512], P('chan')
- grad_w_second: float32 [27, 512, 512], P(None, None, 'chan')
All inputs are finite; a program needn't handle non-finite values.
Results may differ from a plain program's by a relative error of at most 0.005.
Values may be sent and summed in bfloat16 or wider, within the bound.
A program may use at most 64 MiB of HBM per device.

v0:
```python
import math

import jax
import jax.numpy as jnp
from jax import lax
from jax.sharding import PartitionSpec as P

DEPTH = 4
HEIGHT = 16
WIDTH = 16


TAP_OFFSETS = [
    (plane_off, row_off, col_off)
    for plane_off in (-1, 0, 1)
    for row_off in (-1, 0, 1)
    for col_off in (-1, 0, 1)
]
NORM_EPS = 1e-05


def moved_cells(field, plane_off, row_off, col_off):
    cell_count = field.shape[1]
    plane_cells = HEIGHT * WIDTH
    offset = plane_off * plane_cells + row_off * WIDTH + col_off
    margin = plane_cells + WIDTH + 1
    padded = jnp.pad(field, ((0, 0), (margin, margin)))
    sliced = lax.slice_in_dim(padded, margin + offset, margin + offset + cell_count, axis=1)
    cells = jnp.arange(cell_count, dtype=jnp.int32)
    depth_at = cells // plane_cells + plane_off
    row_at = cells // WIDTH % HEIGHT + row_off
    col_at = cells % WIDTH + col_off
    inside = (
        (depth_at >= 0)
        & (depth_at < DEPTH)
        & (row_at >= 0)
        & (row_at < HEIGHT)
        & (col_at >= 0)
        & (col_at < WIDTH)
    )
    return jnp.where(inside[None, :], sliced, jnp.zeros_like(sliced))


def stack_taps(field, sign):
    layers = [
        moved_cells(field, sign * offsets[0], sign * offsets[1], sign * offsets[2])
        for offsets in TAP_OFFSETS
    ]
    return jnp.concatenate(layers, axis=0).reshape(27, field.shape[0], field.shape[1])


def block_rows(count):
    chosen = 1
    for trial in range(1, 65):
        if count % trial == 0:
            chosen = trial
    return chosen


def normalize(pre, gain_rows):
    center = pre - jnp.mean(pre, axis=1, keepdims=True)
    inverse = lax.rsqrt(jnp.mean(center * center, axis=1, keepdims=True) + NORM_EPS)
    normed = center * inverse
    scaled = gain_rows[:, None] * normed
    return (normed, inverse, scaled, jax.nn.silu(scaled).astype(jnp.bfloat16))


def normalize_back(dact, normed, inverse, scaled, gain_rows):
    sigma = jax.nn.sigmoid(scaled)
    dscaled = dact * sigma * (1.0 + scaled * (1.0 - sigma))
    gain_part = jnp.sum(dscaled * normed, axis=1)
    dnormed = dscaled * gain_rows[:, None]
    dpre = (
        dnormed
        - jnp.mean(dnormed, axis=1, keepdims=True)
        - normed * jnp.mean(dnormed * normed, axis=1, keepdims=True)
    ) * inverse
    return (gain_part, dpre.astype(jnp.bfloat16))


def shards(volume, w_first, gain, w_second, cotangent):
    local_rows = volume.shape[1]
    channels_all = w_first.shape[2]
    cell_count = volume.shape[2]
    source = volume[0]
    target = cotangent[0]
    chan_index = lax.axis_index("chan")
    volume_cols = stack_taps(source, 1)
    target_cols = stack_taps(target, -1)
    contract_first = (((0, 1), (0, 1)), ((), ()))
    contract_second = (((0, 2), (0, 1)), ((), ()))
    contract_cells = (((2,), (1,)), ((), ()))
    second_init = (
        jnp.zeros((local_rows, cell_count), jnp.float32),
        jnp.zeros((27, channels_all, local_rows), jnp.float32),
    )
    first_init = (
        jnp.zeros((local_rows, cell_count), jnp.float32),
        jnp.zeros((27, local_rows, channels_all), jnp.float32),
    )
    own_gain = lax.dynamic_slice_in_dim(gain, chan_index * local_rows, local_rows, 0)
    weights = w_first
    pre_own = lax.psum_scatter(
        lax.dot_general(weights, volume_cols, contract_first, preferred_element_type=jnp.float32),
        "chan",
        scatter_dimension=0,
        tiled=True,
    )
    normed, inverse, scaled, act_own = normalize(pre_own, own_gain)
    act_rows = lax.all_gather(act_own, "chan", axis=0, tiled=True)
    count = act_rows.shape[0]
    step_rows = block_rows(count)

    def second_one_block(index, inner):
        out_now, grad_now = inner
        begin = index * step_rows
        rows = lax.dynamic_slice_in_dim(act_rows, begin, step_rows, 0)
        cols = stack_taps(rows, 1)
        weights = lax.dynamic_slice_in_dim(w_second, begin, step_rows, 1)
        out_now = out_now + lax.dot_general(
            weights, cols, contract_first, preferred_element_type=jnp.float32
        )
        grad_part = lax.dot_general(
            cols, target, contract_cells, preferred_element_type=jnp.float32
        )
        grad_now = lax.dynamic_update_slice_in_dim(grad_now, grad_part, begin, 1)
        return (out_now, grad_now)

    out_sum, second_grad = lax.fori_loop(0, count // step_rows, second_one_block, second_init)
    output = out_sum.astype(jnp.bfloat16)[None]
    factor = 1.0 / math.sqrt(lax.axis_size("dp") * cell_count)
    weights = w_second
    dact_own = lax.psum_scatter(
        lax.dot_general(weights, target_cols, contract_second, preferred_element_type=jnp.float32),
        "chan",
        scatter_dimension=0,
        tiled=True,
    )
    gain_part, dpre_own = normalize_back(dact_own, normed, inverse, scaled, own_gain)
    grad_rows = lax.all_gather(dpre_own, "chan", axis=0, tiled=True)
    count = grad_rows.shape[0]
    first_step_rows = block_rows(count)

    def first_one_block(index, inner):
        back_now, grad_now = inner
        begin = index * first_step_rows
        rows = lax.dynamic_slice_in_dim(grad_rows, begin, first_step_rows, 0)
        cols = stack_taps(rows, -1)
        weights = lax.dynamic_slice_in_dim(w_first, begin, first_step_rows, 2)
        back_now = back_now + lax.dot_general(
            weights, cols, contract_second, preferred_element_type=jnp.float32
        )
        grad_part = lax.dot_general(
            volume_cols, rows, contract_cells, preferred_element_type=jnp.float32
        )
        grad_now = lax.dynamic_update_slice_in_dim(grad_now, grad_part, begin, 2)
        return (back_now, grad_now)

    back_sum, first_grad = lax.fori_loop(0, count // first_step_rows, first_one_block, first_init)
    first_total, second_total, gain_total = lax.psum((first_grad, second_grad, gain_part), "dp")
    grad_volume = back_sum.astype(jnp.bfloat16)[None]
    return (output, grad_volume, first_total * factor, gain_total * factor, second_total * factor)


def solution(mesh):
    placed = (
        P("dp", "chan", None),
        P(None, "chan", None),
        P(),
        P(None, None, "chan"),
        P("dp", "chan", None),
    )
    return jax.shard_map(
        shards,
        mesh=mesh,
        in_specs=placed,
        out_specs=(
            P("dp", "chan", None),
            P("dp", "chan", None),
            P(None, "chan", None),
            P("chan"),
            P(None, None, "chan"),
        ),
        check_vma=False,
    )
```

profile of v0, /device:TPU:1, one launch (start us, length us, event | category | flops | bytes accessed | tf_op | source)
XLA Modules:
  0.0 805.1 jit_solution(12205179865725809057)
XLA Ops:
  24.7 1.7 copy-done.3
  26.4 3.4 convolution_bitcast_fusion.4
  29.9 2.9 copy.16
  32.9 6.0 convolution_bitcast_fusion.3
  38.8 2.9 copy.18
  42.5 67.1 %reduce-scatter.7.cloned.1.call-done = f32[64,1024]{1,0:T(8,128)} async-done(((f32[512,1024]{1,0:T(8,128)}), f32[64,1024]{1,0:T(8,128)}) %reduce-scatter.7.cloned.1.call-update) | async-done | bytes 262160 | tf_op jit(solution)/shard_map/reduce_scatter | solution.py:103
  111.9 75.8 %reduce-scatter.9.cloned.1.call-done = f32[64,1024]{1,0:T(8,128)} async-done(((f32[512,1024]{1,0:T(8,128)}), f32[64,1024]{1,0:T(8,128)}) %reduce-scatter.9.cloned.1.call-update) | async-done | bytes 262160 | tf_op jit(solution)/shard_map/reduce_scatter | solution.py:133
  189.2 1.8 multiply_convert_fusion
  191.9 44.4 %all-gather.5.cloned.1.call-done = bf16[512,1024]{1,0:T(8,128)(2,1)} async-done(((bf16[64,1024]{1,0:T(8,128)(2,1)}), bf16[512,1024]{1,0:T(8,128)(2,1)}) %all-gather.5.cloned.1.call-update) | async-done | bytes 1048592 | tf_op jit(solution)/shard_map/all_gather | solution.py:140
  236.3 2.2 broadcast_in_dim.1616
  238.5 272.9 %while.39 = (s32[]{:T(128)}, f32[64,1024]{1,0:T(8,128)S(1)}, f32[27,64,512]{2,1,0:T(8,128)}, bf16[27,64,512]{2,1,0:T(8,128)(2,1)S(1)}, bf16[512,1024]{1,0:T(8,12...) while((s32[]{:T(128)}, f32[64,1024]{1,0:T(8,128)S(1)}, ...), condition=%wide.region_9.10_spmd.clone, body=%wide.region_8.9_spmd.clone.sunk | while | flops 456046592 | bytes 31054024 | solution.py:159
  249.4 1.6 select_dynamic-update-slice_fusion.7
  260.9 3.1 fusion.437
  265.1 5.9 dynamic_update_slice.27
  281.8 1.6 select_dynamic-update-slice_fusion.7
  293.3 3.1 fusion.437
  297.5 9.6 %dynamic_update_slice.27 = f32[27,64,512]{2,1,0:T(8,128)} dynamic-update-slice(f32[27,64,512]{2,1,0:T(8,128)} %get-tuple-element.591, f32[27,64,64]{2,1,0:T(8,128)S(1)} %convolution_bitcast_fusion.6, s32[]{:T(128)} %constant.1758.clone.1..sunk.1, s32[]{:T(128)} %constant.1758.clone.1..sunk.1, s32[]{:T(128)S(6)} %select_n.6693) | dynamic-update-slice | bytes 884740 | tf_op jit(solution)/shard_map/while/body/eval_jaxpr/dynamic_update_slice | solution.py:156
  318.0 1.6 select_dynamic-update-slice_fusion.7
  329.5 3.1 fusion.437
  333.7 5.8 dynamic_update_slice.27
  350.3 1.6 select_dynamic-update-slice_fusion.7
  361.8 3.1 fusion.437
  366.0 9.6 %dynamic_update_slice.27 = f32[27,64,512]{2,1,0:T(8,128)} dynamic-update-slice(f32[27,64,512]{2,1,0:T(8,128)} %get-tuple-element.591, f32[27,64,64]{2,1,0:T(8,128)S(1)} %convolution_bitcast_fusion.6, s32[]{:T(128)} %constant.1758.clone.1..sunk.1, s32[]{:T(128)} %constant.1758.clone.1..sunk.1, s32[]{:T(128)S(6)} %select_n.6693) | dynamic-update-slice | bytes 884740 | tf_op jit(solution)/shard_map/while/body/eval_jaxpr/dynamic_update_slice | solution.py:156
  386.5 1.6 select_dynamic-update-slice_fusion.7
  398.0 3.1 fusion.437
  402.2 5.8 dynamic_update_slice.27
  418.9 1.6 select_dynamic-update-slice_fusion.7
  430.4 3.1 fusion.437
  434.6 9.6 %dynamic_update_slice.27 = f32[27,64,512]{2,1,0:T(8,128)} dynamic-update-slice(f32[27,64,512]{2,1,0:T(8,128)} %get-tuple-element.591, f32[27,64,64]{2,1,0:T(8,128)S(1)} %convolution_bitcast_fusion.6, s32[]{:T(128)} %constant.1758.clone.1..sunk.1, s32[]{:T(128)} %constant.1758.clone.1..sunk.1, s32[]{:T(128)S(6)} %select_n.6693) | dynamic-update-slice | bytes 884740 | tf_op jit(solution)/shard_map/while/body/eval_jaxpr/dynamic_update_slice | solution.py:156
  455.1 1.6 select_dynamic-update-slice_fusion.7
  466.6 3.1 fusion.437
  470.8 5.2 dynamic_update_slice.27
  498.4 3.1 fusion.437
  502.6 8.8 %dynamic_update_slice.27 = f32[27,64,512]{2,1,0:T(8,128)} dynamic-update-slice(f32[27,64,512]{2,1,0:T(8,128)} %get-tuple-element.591, f32[27,64,64]{2,1,0:T(8,128)S(1)} %convolution_bitcast_fusion.6, s32[]{:T(128)} %constant.1758.clone.1..sunk.1, s32[]{:T(128)} %constant.1758.clone.1..sunk.1, s32[]{:T(128)S(6)} %select_n.6693) | dynamic-update-slice | bytes 884740 | tf_op jit(solution)/shard_map/while/body/eval_jaxpr/dynamic_update_slice | solution.py:156
  511.4 2.2 broadcast_in_dim.1587
  513.7 139.8 %while.38 = (s32[]{:T(128)}, f32[64,1024]{1,0:T(8,128)}, f32[27,512,64]{1,2,0:T(8,128)}, bf16[27,512,64]{1,2,0:T(8,128)(2,1)}, bf16[512,1024]{1,0:T(8,128)(2,1)}...) while((s32[]{:T(128)}, f32[64,1024]{1,0:T(8,128)}, ...), condition=%wide.region_4.5_spmd.clone, body=%wide.region_3.4_spmd.clone.sunk | while | flops 456046592 | bytes 17422536 | solution.py:129
  518.6 2.7 fusion.406
  521.3 6.1 dynamic_update_slice.26
  527.4 2.6 fusion.405
  534.9 2.7 fusion.406
  537.6 8.5 %dynamic_update_slice.26 = f32[27,512,64]{1,2,0:T(8,128)} dynamic-update-slice(f32[27,512,64]{1,2,0:T(8,128)} %get-tuple-element.561, f32[27,64,64]{1,2,0:T(8,128)} %fusion.406, s32[]{:T(128)} %constant.1758.clone.1..sunk, s32[]{:T(128)S(6)} %select_n.6557, s32[]{:T(128)} %constant.1758.clone.1..sunk) | dynamic-update-slice | bytes 884740 | tf_op jit(solution)/shard_map/while/body/eval_jaxpr/dynamic_update_slice | solution.py:126
  546.2 2.7 fusion.405
  553.8 2.7 fusion.406
  556.5 6.1 dynamic_update_slice.26
  562.6 2.7 fusion.405
  570.3 2.7 fusion.406
  573.0 8.5 %dynamic_update_slice.26 = f32[27,512,64]{1,2,0:T(8,128)} dynamic-update-slice(f32[27,512,64]{1,2,0:T(8,128)} %get-tuple-element.561, f32[27,64,64]{1,2,0:T(8,128)} %fusion.406, s32[]{:T(128)} %constant.1758.clone.1..sunk, s32[]{:T(128)S(6)} %select_n.6557, s32[]{:T(128)} %constant.1758.clone.1..sunk) | dynamic-update-slice | bytes 884740 | tf_op jit(solution)/shard_map/while/body/eval_jaxpr/dynamic_update_slice | solution.py:126
  581.5 2.7 fusion.405
  589.2 2.7 fusion.406
  591.9 6.1 dynamic_update_slice.26
  598.0 2.7 fusion.405
  605.6 2.7 fusion.406
  608.3 8.5 %dynamic_update_slice.26 = f32[27,512,64]{1,2,0:T(8,128)} dynamic-update-slice(f32[27,512,64]{1,2,0:T(8,128)} %get-tuple-element.561, f32[27,64,64]{1,2,0:T(8,128)} %fusion.406, s32[]{:T(128)} %constant.1758.clone.1..sunk, s32[]{:T(128)S(6)} %select_n.6557, s32[]{:T(128)} %constant.1758.clone.1..sunk) | dynamic-update-slice | bytes 884740 | tf_op jit(solution)/shard_map/while/body/eval_jaxpr/dynamic_update_slice | solution.py:126
  616.9 2.7 fusion.405
  624.5 2.7 fusion.406
  627.2 5.4 dynamic_update_slice.26
  632.6 2.7 fusion.405
  640.2 2.7 fusion.406
  643.0 7.7 dynamic_update_slice.26
  650.7 2.7 fusion.405
  653.4 28.7 %psum.22 = f32[64]{0:T(128)S(1)} all-reduce(f32[64]{0:T(128)S(1)} %get-tuple-element.439), channel_id=1, replica_groups=mesh['dp'=16,'chan'=8] {'dp'}, use_global_device_ids=true, to_apply=%region_12.13 | all-reduce | flops 64 | bytes 512 | tf_op jit(solution)/shard_map/psum | solution.py:160
  684.0 107.8 %all-reduce.7.cloned.1.call-done = (f32[27,64,512]{2,1,0:T(8,128)}, f32[27,512,64]{1,2,0:T(8,128)}) async-done(((f32[27,64,512]{2,1,0:T(8,128)}, f32[27,512,64]{1,2,0:T(8,128)}), (f32[27,64,512]{2,1,0:T(8,128)}, f32[27,512,64]{1,2,0:T(8,128)})) %all-reduce.7.cloned.1.call-update) | async-done | bytes 7077904 | tf_op jit(solution)/shard_map/psum | solution.py:160
  791.7 4.6 broadcast_multiply_fusion
  796.3 2.2 broadcast_multiply_fusion.1
  (1033 shorter events, 237.1 us)
Async XLA Ops:
  7.2 13.5 %copy-start = (bf16[1,64,1024]{2,1,0:T(8,128)(2,1)S(1)}, bf16[1,64,1024]{2,1,0:T(8,128)(2,1)}, u32[]{:S(2)}) copy-start(bf16[1,64,1024]{2,1,0:T(8,128)(2,1)} %param.13) | copy-start | bytes 393220
  7.2 14.7 %copy-start.2 = (bf16[1,64,1024]{2,1,0:T(8,128)(2,1)S(1)}, bf16[1,64,1024]{2,1,0:T(8,128)(2,1)}, u32[]{:S(2)}) copy-start(bf16[1,64,1024]{2,1,0:T(8,128)(2,1)} %param.9) | copy-start | bytes 393220
  7.2 102.5 %reduce-scatter.7.cloned.1.call-start = ((), (), s32[]{:S(2)}) async-start(), calls=%async_computation.4 | async-start | bytes 2359296 | tf_op jit(solution)/shard_map/reduce_scatter | solution.py:103
  22.0 2.6 copy-start.10
  22.1 4.4 copy-start.9
  24.7 1.8 copy-start.3
  32.8 154.9 %reduce-scatter.9.cloned.1.call-start = ((), (), s32[]{:S(2)}) async-start(), calls=%async_computation.5 | async-start | bytes 2359296 | tf_op jit(solution)/shard_map/reduce_scatter | solution.py:133
  41.7 194.6 %all-gather.5.cloned.1.call-start = ((), (), s32[]{:S(2)}) async-start(), calls=%async_computation.3 | async-start | bytes 1179648 | tf_op jit(solution)/shard_map/all_gather | solution.py:140
  191.0 320.4 %all-gather.3.cloned.1.call-start = ((), (), s32[]{:S(2)}) async-start(), calls=%async_computation.2 | async-start | bytes 1179648 | tf_op jit(solution)/shard_map/all_gather | solution.py:110
  191.6 600.1 %all-reduce.7.cloned.1.call-start = ((), (), s32[]{:S(2)}) async-start(), calls=%async_computation.6 | async-start | bytes 14155776 | tf_op jit(solution)/shard_map/psum | solution.py:160
  260.9 3.1 copy-start.4
  293.3 3.1 copy-start.4
  329.5 3.1 copy-start.4
  361.8 3.1 copy-start.4
  398.0 3.1 copy-start.4
  430.4 3.1 copy-start.4
  466.6 3.1 copy-start.4
  498.4 3.1 copy-start.4
  511.4 2.2 copy-start.6
  514.6 4.0 copy-start.1
  530.9 4.0 copy-start.1
  549.8 4.0 copy-start.1
  566.3 4.0 copy-start.1
  585.2 4.0 copy-start.1
  601.6 4.0 copy-start.1
  620.5 4.0 copy-start.1
  636.2 4.0 copy-start.1
  653.4 29.2 %copy-start.7 = (f32[64,1024]{1,0:T(8,128)S(1)}, f32[64,1024]{1,0:T(8,128)}, u32[]{:S(2)}) copy-start(f32[64,1024]{1,0:T(8,128)} %copy-done.6) | copy-start | bytes 786436
  653.4 29.9 %copy-start.5 = (f32[64,1024]{1,0:T(8,128)S(1)}, f32[64,1024]{1,0:T(8,128)}, u32[]{:S(2)}) copy-start(f32[64,1024]{1,0:T(8,128)} %get-tuple-element.381) | copy-start | bytes 786436
  791.7 4.6 copy-start.8
Sparse Core Ops, SparseCore 0:
  32.9 76.6 reduce-scatter.6
  114.0 73.7 reduce-scatter.8
  191.2 45.0 all-gather.4
  239.1 45.0 all-gather.2
  653.6 138.1 all-reduce.6
where the time goes:
time: 809 us; the launch traced here: 805 us
  waiting for transfers between devices  296 us (37%)
  other arithmetic  232 us (29%)
  local copies, waits for them, and re-layouts  145 us (18%)
  matrix products  86.1 us (11%)
  blocking collectives  28.7 us (4%)
  between operations  14.4 us (2%)
    while x416, other arithmetic  189 us
    psum x1, waiting for transfers between devices, shards(): lax.psum((first_grad, second_grad, gain_part), 'dp')  108 us
    reduce_scatter x1, waiting for transfers between devices, shards(): lax.psum_scatter(lax.dot_general(weights, target_cols, contract_second, p...  75.8 us
    reduce_scatter x1, waiting for transfers between devices, shards(): lax.psum_scatter(lax.dot_general(weights, volume_cols, contract_first, pr...  67.1 us
    dynamic_update_slice x8, local copies, waits for them, and re-layouts, first_one_block(): grad_now = lax.dynamic_update_slice_in_dim(grad_now, grad_part, begin, 2)  60.5 us
    dynamic_update_slice x8, local copies, waits for them, and re-layouts, second_one_block(): grad_now = lax.dynamic_update_slice_in_dim(grad_now, grad_part, begin, 1)  56.9 us
    all_gather x1, waiting for transfers between devices, shards(): grad_rows = lax.all_gather(dpre_own, 'chan', axis=0, tiled=True)  44.4 us
    psum x1, blocking collectives, shards(): lax.psum((first_grad, second_grad, gain_part), 'dp')  28.7 us
  transfers between devices with their start and end apart: 5, of which 4 were waited for; matrix products, arithmetic and copies ran while one was open for 36% of the time, Pallas kernels for 0%

commit v1 on v0

v1 whole, which is shorter than its diff:
```python
import math

import jax
import jax.numpy as jnp
from jax import lax
from jax.experimental import pallas as pl
from jax.experimental.pallas import tpu as pltpu
from jax.sharding import PartitionSpec as P

NORM_EPS = 1e-05
PLANES, ROWS, COLS = 4, 16, 16
PLANE = ROWS * COLS
CELLS = PLANES * PLANE
OWN = 64
ALL = 512
TAPS = 27
TALL = TAPS * OWN
ZBLOCK = TALL // 4
HALF = ALL // 2
QUART = ALL // 4
MESH = pl.DeviceIdType.MESH
F32 = jnp.float32
BF16 = jnp.bfloat16


def inside(shape, row_off, col_off):
    cell = lax.broadcasted_iota(jnp.int32, shape, 1)
    row = cell // COLS % ROWS + row_off
    col = cell % COLS + col_off
    return (row >= 0) & (row < ROWS) & (col >= 0) & (col < COLS)


def moved(field, row_off, col_off):
    offset = row_off * COLS + col_off
    if offset == 0:
        return field
    rolled = pltpu.roll(field, (-offset) % CELLS, axis=1)
    return jnp.where(inside(field.shape, row_off, col_off), rolled, 0.0)


def build_columns(src, dst, sign):
    field = src[...].astype(F32)
    blank = jnp.zeros((OWN, PLANE), BF16)
    for b in (-1, 0, 1):
        for c in (-1, 0, 1):
            block = moved(field, sign * b, sign * c).astype(BF16)
            for a in (-1, 0, 1):
                tap = 9 * (a + 1) + 3 * (b + 1) + c + 1
                rows = pl.ds(tap * OWN, OWN)
                step = sign * a
                if step == 0:
                    dst[rows, :] = block
                elif step > 0:
                    dst[rows, 0 : CELLS - PLANE] = block[:, PLANE:]
                    dst[rows, CELLS - PLANE : CELLS] = blank
                else:
                    dst[rows, PLANE:CELLS] = block[:, : CELLS - PLANE]
                    dst[rows, 0:PLANE] = blank


def turn(src, dst):
    def one(index, carry):
        at = pl.multiple_of(index * 128, 128)
        dst[:, pl.ds(at, 128)] = src[pl.ds(at, 128), :].T
        return carry

    lax.fori_loop(0, TALL // 128, one, 0)
    rest = TALL // 128 * 128
    dst[:, rest:TALL] = src[rest:TALL, :].T


def partial_sums(turned, columns, dst, first, last):
    def one(index, carry):
        at = pl.multiple_of(index * PLANE, PLANE)
        dst[:, pl.ds(at, PLANE)] = jnp.dot(
            turned[...], columns[:, pl.ds(at, PLANE)], preferred_element_type=F32
        ).astype(BF16)
        return carry

    lax.fori_loop(first, last, one, 0)


def conv_out(weights, gathered, wide, dst, sign):
    nine = 9 * OWN
    for d in range(PLANES):
        total = None
        for a in (-1, 0, 1):
            plane = d + sign * a
            if plane < 0 or plane >= PLANES:
                continue
            term = jnp.dot(
                weights[pl.ds((a + 1) * nine, nine), :],
                gathered[:, pl.ds(plane * PLANE, PLANE)],
                preferred_element_type=F32,
            )
            total = term if total is None else total + term
        wide[:, pl.ds(d * PLANE, PLANE)] = total

    def one(index, carry):
        at = pl.multiple_of(index * 16, 16)
        total = jnp.zeros((16, CELLS), F32)
        for b in (-1, 0, 1):
            for c in (-1, 0, 1):
                tap = 3 * (b + 1) + c + 1
                total = total + moved(wide[pl.ds(tap * OWN + at, 16), :], sign * b, sign * c)
        dst[pl.ds(at, 16), :] = total.astype(BF16)
        return carry

    lax.fori_loop(0, OWN // 16, one, 0)


def kernel(
    volume, w_first, gain, w_second, cotangent,
    output, grad_volume, grad_first, grad_gain, grad_second,
    vol_cols, cot_cols, turned, sums_a, sums_b, got_a, got_b, act, dpre,
    normed, sigma, inverse, wide,
    core_out_a, core_in_a, z_out_a, z_in_a, keep_a, x_out_a, x_in_a,
    core_out_b, core_in_b, z_out_b, z_in_b, keep_b, x_out_b, x_in_b,
    gain_core, gain_z, gain_x, send_sems, recv_sems,
):
    dp = lax.axis_index("dp")
    chan = lax.axis_index("chan")
    x_lo, z, core = dp // 8, dp // 2 % 4, dp % 2
    y, x_hi = chan // 2, chan % 2
    count = [0]

    def send(src, dst, device):
        index = count[0]
        count[0] += 1
        copy = pltpu.make_async_remote_copy(
            src_ref=src,
            dst_ref=dst,
            send_sem=send_sems.at[index],
            recv_sem=recv_sems.at[index],
            device_id=device,
            device_id_type=MESH,
        )
        copy.start()
        pending.append(copy)
        return copy

    pending = []
    peers = []
    for k in (4, 2, 6, 1, 5, 3, 7):
        other = (y + k // 2) % 4 * 2 + (x_hi + k % 2) % 2
        peers.append((other, (dp, other)))
    core_peer = (x_lo * 8 + z * 2 + 1 - core, chan)
    x_peer = ((1 - x_lo) * 8 + z * 2 + core, chan)
    z_peer = {j: (x_lo * 8 + (z + j) % 4 * 2 + core, chan) for j in (1, 2, 3)}

    barrier = pltpu.get_barrier_semaphore()
    everyone = [device for _, device in peers] + [core_peer, x_peer] + list(z_peer.values())
    for device in everyone:
        pl.semaphore_signal(barrier, inc=1, device_id=device, device_id_type=MESH)

    def scatter(sums, got, first, width):
        copies = []
        cells = pl.ds(first, width)
        for slot, (other, device) in enumerate(peers):
            rows = pl.ds(pl.multiple_of(other * OWN, OWN), OWN)
            copies.append(send(sums.at[rows, cells], got.at[slot, :, cells], device))
        return copies

    def share(block):
        rows = pl.ds(pl.multiple_of(chan * OWN, OWN), OWN)
        return [send(block.at[rows, :], block.at[rows, :], device) for _, device in peers]

    def arrived(copies):
        for copy in copies:
            copy.wait_recv()

    build_columns(volume, vol_cols, 1)
    turn(w_first, turned)
    partial_sums(turned, vol_cols, sums_a, 0, 2)
    pl.semaphore_wait(barrier, len(everyone))
    first_sums = scatter(sums_a, got_a, 0, CELLS // 2)
    partial_sums(turned, vol_cols, sums_a, 2, 4)
    first_sums += scatter(sums_a, got_a, CELLS // 2, CELLS // 2)

    build_columns(cotangent, cot_cols, -1)
    turn(w_second, turned)
    partial_sums(turned, cot_cols, sums_b, 0, 2)
    second_sums = scatter(sums_b, got_b, 0, CELLS // 2)
    partial_sums(turned, cot_cols, sums_b, 2, 4)

    place = lax.broadcasted_iota(jnp.int32, (OWN, ALL), 1)
    wanted = lax.broadcasted_iota(jnp.int32, (OWN, ALL), 0) + chan * OWN
    gain_own = jnp.sum(
        jnp.where(place == wanted, jnp.broadcast_to(gain[...], (OWN, ALL)), 0.0),
        axis=1,
        keepdims=True,
    )
    scale = 1.0 / CELLS

    def summed(sums, got, at):
        total = sums[pl.ds(pl.multiple_of(chan * OWN + at, 16), 16), :].astype(F32)
        for slot in range(7):
            total = total + got[slot, pl.ds(at, 16), :].astype(F32)
        return total

    arrived(first_sums)
    for group in range(OWN // 16):
        at = group * 16
        gain_rows = gain_own[at : at + 16]
        pre = summed(sums_a, got_a, at)
        center = pre - jnp.sum(pre, axis=1, keepdims=True) * scale
        inv = lax.rsqrt(jnp.sum(center * center, axis=1, keepdims=True) * scale + NORM_EPS)
        unit = center * inv
        scaled = gain_rows * unit
        sig = jax.nn.sigmoid(scaled)
        normed[pl.ds(at, 16), :] = unit
        sigma[pl.ds(at, 16), :] = sig
        inverse[pl.ds(at, 16), :] = jnp.broadcast_to(inv, (16, 128))
        act[pl.ds(pl.multiple_of(chan * OWN + at, 16), 16), :] = (scaled * sig).astype(BF16)
    act_copies = share(act)
    second_sums += scatter(sums_b, got_b, CELLS // 2, CELLS // 2)

    arrived(second_sums)
    gain_row = jnp.zeros((8, 128), F32)
    for group in range(OWN // 16):
        at = group * 16
        gain_rows = gain_own[at : at + 16]
        dact = summed(sums_b, got_b, at)
        unit = normed[pl.ds(at, 16), :]
        sig = sigma[pl.ds(at, 16), :]
        inv = inverse[pl.ds(at, 16), 0:1]
        scaled = gain_rows * unit
        dscaled = dact * sig * (1.0 + scaled * (1.0 - sig))
        part = jnp.sum(dscaled * unit, axis=1, keepdims=True)
        spot = lax.broadcasted_iota(jnp.int32, (16, 128), 1)
        here = lax.broadcasted_iota(jnp.int32, (16, 128), 0) + at
        row = jnp.sum(jnp.where(spot == here, part, 0.0), axis=0, keepdims=True)
        gain_row = gain_row + jnp.broadcast_to(row, (8, 128))
        dnormed = dscaled * gain_rows
        mean_d = jnp.sum(dnormed, axis=1, keepdims=True) * scale
        mean_u = jnp.sum(dnormed * unit, axis=1, keepdims=True) * scale
        back = (dnormed - mean_d - unit * mean_u) * inv
        dpre[pl.ds(pl.multiple_of(chan * OWN + at, 16), 16), :] = back.astype(BF16)
    dpre_copies = share(dpre)
    gain_core[0] = gain_row
    gain_core_copy = send(gain_core.at[0], gain_core.at[1], core_peer)

    order = (2, 1, 3, 0)

    def z_rows(j):
        return pl.ds(pl.multiple_of((z + j) % 4 * ZBLOCK, ZBLOCK), ZBLOCK)

    def against(columns, gathered, rows, side):
        half = gathered[pl.ds(pl.multiple_of(side * HALF, HALF), HALF), :]
        return lax.dot_general(
            columns[rows, :], half, (((1,), (1,)), ((), ())), preferred_element_type=F32
        )

    def reduce_start(columns, gathered, core_out, core_in, z_out, z_in, keep):
        crossing = {}
        for j in order:
            core_out[j] = against(columns, gathered, z_rows(j), 1 - core).astype(BF16)
            crossing[j] = send(core_out.at[j], core_in.at[j], core_peer)
        z_copies = []
        for j in order:
            mine = against(columns, gathered, z_rows(j), core)
            crossing[j].wait_recv()
            mine = mine + core_in[j].astype(F32)
            if j == 0:
                keep[...] = mine
            else:
                z_out[j - 1] = mine.astype(BF16)
                z_copies.append(send(z_out.at[j - 1], z_in.at[j - 1], z_peer[j]))
        return z_copies

    def lanes(side):
        return pl.ds(pl.multiple_of(side * QUART, QUART), QUART)

    def reduce_x(z_copies, z_in, keep, x_out, x_in):
        arrived(z_copies)
        keep[...] = keep[...] + z_in[0].astype(F32) + z_in[1].astype(F32) + z_in[2].astype(F32)
        x_out[...] = keep[:, lanes(1 - x_lo)].astype(BF16)
        return send(x_out, x_in, x_peer)

    factor = 1.0 / math.sqrt(lax.axis_size("dp") * CELLS)

    def spread_x(x_copy, keep, x_in, final):
        x_copy.wait_recv()
        rows = z_rows(0)
        mine = lanes(core * 2 + x_lo)
        final[rows, mine] = ((keep[:, lanes(x_lo)] + x_in[...].astype(F32)) * factor).astype(BF16)
        spot = final.at[rows, mine]
        to_x = send(spot, spot, x_peer)
        return to_x, {j: [send(spot, spot, z_peer[j])] for j in (2, 1, 3)}

    def spread_z(spread, final):
        to_x, to_z = spread
        to_x.wait_recv()
        rows = z_rows(0)
        spot = final.at[rows, lanes(core * 2 + 1 - x_lo)]
        for j in (2, 1, 3):
            to_z[j].append(send(spot, spot, z_peer[j]))
        whole = final.at[rows, pl.ds(pl.multiple_of(core * HALF, HALF), HALF)]
        return to_z, [send(whole, whole, core_peer)]

    def spread_core(state, final):
        to_z, to_core = state
        for j in (1, 3, 2):
            arrived(to_z[j])
            whole = final.at[z_rows(4 - j), pl.ds(pl.multiple_of(core * HALF, HALF), HALF)]
            to_core.append(send(whole, whole, core_peer))
        return to_core

    arrived(act_copies)
    z_second = reduce_start(cot_cols, act, core_out_b, core_in_b, z_out_b, z_in_b, keep_b)
    conv_out(w_second, act, wide, output, 1)

    arrived(dpre_copies)
    gain_core_copy.wait_recv()
    gain_mine = gain_core[0] + gain_core[1]
    gain_z[z] = gain_mine
    gain_copies = [send(gain_z.at[z], gain_z.at[z], z_peer[j]) for j in (1, 2, 3)]
    z_first = reduce_start(vol_cols, dpre, core_out_a, core_in_a, z_out_a, z_in_a, keep_a)

    x_second = reduce_x(z_second, z_in_b, keep_b, x_out_b, x_in_b)
    arrived(gain_copies)
    gain_x[0] = (gain_z[0] + gain_z[1]) + (gain_z[2] + gain_z[3])
    gain_x_copy = send(gain_x.at[0], gain_x.at[1], x_peer)
    second_spread = spread_x(x_second, keep_b, x_in_b, grad_second)
    second_state = spread_z(second_spread, grad_second)
    conv_out(w_first, dpre, wide, grad_volume, -1)
    x_first = reduce_x(z_first, z_in_a, keep_a, x_out_a, x_in_a)
    first_spread = spread_x(x_first, keep_a, x_in_a, grad_first)
    first_state = spread_z(first_spread, grad_first)
    last = spread_core(second_state, grad_second)
    gain_x_copy.wait_recv()
    grad_gain[...] = (gain_x[0] + gain_x[1]) * factor
    last += spread_core(first_state, grad_first)
    arrived(last)
    for copy in pending:
        copy.wait_send()


def shards(volume, w_first, gain, w_second, cotangent):
    vmem = pl.BlockSpec(memory_space=pltpu.VMEM)
    shape = jax.ShapeDtypeStruct
    reducing = [
        pltpu.VMEM((4, ZBLOCK, HALF), BF16),
        pltpu.VMEM((4, ZBLOCK, HALF), BF16),
        pltpu.VMEM((3, ZBLOCK, HALF), BF16),
        pltpu.VMEM((3, ZBLOCK, HALF), BF16),
        pltpu.VMEM((ZBLOCK, HALF), F32),
        pltpu.VMEM((ZBLOCK, QUART), BF16),
        pltpu.VMEM((ZBLOCK, QUART), BF16),
    ]
    output, grad_volume, grad_first, grad_gain, grad_second = pl.pallas_call(
        kernel,
        name="conv_pair",
        out_shape=(
            shape((OWN, CELLS), BF16),
            shape((OWN, CELLS), BF16),
            shape((TALL, ALL), BF16),
            shape((8, 128), F32),
            shape((TALL, ALL), BF16),
        ),
        in_specs=[vmem] * 5,
        out_specs=[vmem] * 5,
        scratch_shapes=[
            pltpu.VMEM((TALL, CELLS), BF16),
            pltpu.VMEM((TALL, CELLS), BF16),
            pltpu.VMEM((ALL, TALL), BF16),
            pltpu.VMEM((ALL, CELLS), BF16),
            pltpu.VMEM((ALL, CELLS), BF16),
            pltpu.VMEM((7, OWN, CELLS), BF16),
            pltpu.VMEM((7, OWN, CELLS), BF16),
            pltpu.VMEM((ALL, CELLS), BF16),
            pltpu.VMEM((ALL, CELLS), BF16),
            pltpu.VMEM((OWN, CELLS), F32),
            pltpu.VMEM((OWN, CELLS), F32),
            pltpu.VMEM((OWN, 128), F32),
            pltpu.VMEM((9 * OWN, CELLS), F32),
        ]
        + reducing
        + reducing
        + [
            pltpu.VMEM((2, 8, 128), F32),
            pltpu.VMEM((4, 8, 128), F32),
            pltpu.VMEM((2, 8, 128), F32),
            pltpu.SemaphoreType.DMA((96,)),
            pltpu.SemaphoreType.DMA((96,)),
        ],
        compiler_params=pltpu.CompilerParams(
            collective_id=0, has_side_effects=True, vmem_limit_bytes=60 << 20
        ),
    )(
        volume[0],
        w_first.reshape(TALL, ALL),
        gain.reshape(1, ALL),
        w_second.transpose(0, 2, 1).reshape(TALL, ALL),
        cotangent[0],
    )
    return (
        output[None],
        grad_volume[None],
        grad_first.astype(F32).reshape(TAPS, OWN, ALL),
        grad_gain[0, :OWN],
        grad_second.astype(F32).reshape(TAPS, OWN, ALL).transpose(0, 2, 1),
    )


def solution(mesh):
    placed = (
        P("dp", "chan", None),
        P(None, "chan", None),
        P(),
        P(None, None, "chan"),
        P("dp", "chan", None),
    )
    return jax.shard_map(
        shards,
        mesh=mesh,
        in_specs=placed,
        out_specs=(
            P("dp", "chan", None),
            P("dp", "chan", None),
            P(None, "chan", None),
            P("chan"),
            P(None, None, "chan"),
        ),
        check_vma=False,
    )
```

time: 809 us -> 109 us (0.13)
  waiting for transfers between devices: 296 us -> 0 us
  other arithmetic: 232 us -> 6.16 us
  local copies, waits for them, and re-layouts: 145 us -> 2.51 us
  Pallas kernels: 0 us -> 99.9 us
  matrix products: 86.1 us -> 0 us
  blocking collectives: 28.7 us -> 0 us
  between operations: 14.4 us -> 0.65 us
    while x416 -> x0, other arithmetic: 189 us -> none
    reduce_scatter x2 -> x0, waiting for transfers between devices: 143 us -> none  [the longest x1 75.8 us: shards(): lax.psum_scatter(lax.dot_general(weights, target_cols, contract_second, p...]
    dynamic_update_slice x16 -> x0, local copies, waits for them, and re-layouts: 117 us -> none  [the longest x8 60.5 us: first_one_block(): grad_now = lax.dynamic_update_slice_in_dim(grad_now, grad_part, begin, 2)]
    psum x1 -> x0, waiting for transfers between devices: 108 us -> none  [shards(): lax.psum((first_grad, second_grad, gain_part), 'dp')]
    pallas_call x0 -> x1, Pallas kernels: none -> 99.9 us  [shards(): pl.pallas_call(kernel, name='conv_pair', out_shape=(shape((OWN, CELLS), B...]
    dot_general x34 -> x0, matrix products: 86.1 us -> none  [the longest x8 24.7 us: first_one_block(): lax.dot_general(weights, cols, contract_second, preferred_element_type=jn...]
    all_gather x2 -> x0, waiting for transfers between devices: 44.4 us -> none  [the longest x1 44.4 us: shards(): grad_rows = lax.all_gather(dpre_own, 'chan', axis=0, tiled=True)]
    psum x1 -> x0, blocking collectives: 28.7 us -> none  [shards(): lax.psum((first_grad, second_grad, gain_part), 'dp')]
  transfers between devices with their start and end apart: 5 -> 0, of which waited for: 4 -> 0; matrix products, arithmetic and copies ran while one was open for 36% -> 0% of each run, Pallas kernels for 0% -> 0%
where the time goes in v1:
time: 109 us
  Pallas kernels  99.9 us (92%)
  other arithmetic  6.16 us (6%)
  local copies, waits for them, and re-layouts  2.51 us (2%)
    pallas_call x1, Pallas kernels, shards(): pl.pallas_call(kernel, name='conv_pair', out_shape=(shape((OWN, CELLS), B...  99.9 us
    reshape x1, other arithmetic, shards(): grad_first.astype(F32).reshape(TAPS, OWN, ALL)  3.88 us
    transpose x1, other arithmetic, shards(): grad_second.astype(F32).reshape(TAPS, OWN, ALL).transpose(0, 2, 1)  2.28 us

profile of v1, /device:TPU:1, one launch (start us, length us, event | category | flops | bytes accessed | tf_op | source)
XLA Modules:
  0.0 109.3 jit_solution(3587677447345797370)
XLA Ops:
  0.6 99.9 %conv_pair.1 = (bf16[64,1024]{1,0:T(8,128)(2,1)}, bf16[64,1024]{1,0:T(8,128)(2,1)}, bf16[1728,512]{1,0:T(8,128)(2,1)}, f32[8,128]{1,0:T(8,128)}, bf16[1728,512]{1,0:T(8,128)(2,1)}) custom-call(bf16[64,1024]{1,0:T(8,128)(2,1)} %bitcast.21, bf16[1728,512]{1,0:T(8,128)(2,1)} %bitcast.17, f32[1,512]{1,0:T(1,128)} %bitcast.25, bf16[1728,512]{1,0:T(8,128)(2,1)} %bitcast.18, ...), custom_call_target="tpu_custom_call" | custom-call | tf_op jit(solution)/shard_map/conv_pair/pallas_call | solution.py:351
  100.6 1.2 %slice_bitcast_fusion = f32[64]{0:T(128)} fusion(f32[8,128]{1,0:T(8,128)} %get-tuple-element.13), kind=kLoop, calls=%fused_computation.1 | loop fusion | bytes 512 | tf_op jit(solution)/shard_map/squeeze | solution.py:401
  101.8 0.0 copy-start
  101.8 3.9 %convert.3 = f32[27,64,512]{2,1,0:T(8,128)} convert(bf16[27,64,512]{2,1,0:T(8,128)(2,1)} %bitcast.20) | non-fusion elementwise | flops 884736 | bytes 5308416 | tf_op jit(solution)/shard_map/reshape | solution.py:400
  105.7 0.0 copy-done
  105.7 0.0 copy-start.2
  105.7 0.0 copy-start.1
  105.7 2.3 %convert_bitcast_fusion = f32[27,512,64]{1,2,0:T(8,128)} fusion(bf16[27,64,512]{2,1,0:T(8,128)(2,1)S(1)} %bitcast.19), kind=kLoop, calls=%fused_computation | loop fusion | flops 884736 | bytes 5308416 | tf_op jit(solution)/shard_map/transpose | solution.py:402
  107.9 0.0 copy-done.2
  107.9 0.7 copy.12
  108.6 0.0 copy-done.1
  108.6 0.7 copy.13
Async XLA Ops:
  101.8 3.9 %copy-start = (bf16[1728,512]{1,0:T(8,128)(2,1)S(1)}, bf16[1728,512]{1,0:T(8,128)(2,1)}, u32[]{:S(2)}) copy-start(bf16[1728,512]{1,0:T(8,128)(2,1)} %get-tuple-element.14) | copy-start | bytes 5308420
  105.7 2.3 %copy-start.2 = (bf16[64,1024]{1,0:T(8,128)(2,1)S(1)}, bf16[64,1024]{1,0:T(8,128)(2,1)}, u32[]{:S(2)}) copy-start(bf16[64,1024]{1,0:T(8,128)(2,1)} %get-tuple-element.10) | copy-start | bytes 393220
  105.7 2.9 %copy-start.1 = (bf16[64,1024]{1,0:T(8,128)(2,1)S(1)}, bf16[64,1024]{1,0:T(8,128)(2,1)}, u32[]{:S(2)}) copy-start(bf16[64,1024]{1,0:T(8,128)(2,1)} %get-tuple-element.11) | copy-start | bytes 393220

commit v2 on v1

v2 whole, which is shorter than its diff:
```python
import math

import jax
import jax.numpy as jnp
from jax import lax
from jax.experimental import pallas as pl
from jax.experimental.pallas import tpu as pltpu
from jax.sharding import PartitionSpec as P

NORM_EPS = 1e-05
PLANES, ROWS, COLS = 4, 16, 16
PLANE = ROWS * COLS
CELLS = PLANES * PLANE
OWN = 64
ALL = 512
TAPS = 27
TALL = TAPS * OWN
ZBLOCK = TALL // 4
HALF = ALL // 2
QUART = ALL // 4
RUN = 32
MESH = pl.DeviceIdType.MESH
F32 = jnp.float32
BF16 = jnp.bfloat16


def inside(shape, row_off, col_off):
    cell = lax.broadcasted_iota(jnp.int32, shape, 1)
    row = cell // COLS % ROWS + row_off
    col = cell % COLS + col_off
    return (row >= 0) & (row < ROWS) & (col >= 0) & (col < COLS)


def moved(field, row_off, col_off):
    offset = row_off * COLS + col_off
    if offset == 0:
        return field
    rolled = pltpu.roll(field, (-offset) % CELLS, axis=1)
    return jnp.where(inside(field.shape, row_off, col_off), rolled, 0.0)


def build_columns(src, dst, sign):
    field = src[...].astype(F32)
    blank = jnp.zeros((OWN, PLANE), BF16)
    for b in (-1, 0, 1):
        for c in (-1, 0, 1):
            block = moved(field, sign * b, sign * c).astype(BF16)
            for a in (-1, 0, 1):
                tap = 9 * (a + 1) + 3 * (b + 1) + c + 1
                rows = pl.ds(tap * OWN, OWN)
                step = sign * a
                if step == 0:
                    dst[rows, :] = block
                elif step > 0:
                    dst[rows, 0 : CELLS - PLANE] = block[:, PLANE:]
                    dst[rows, CELLS - PLANE : CELLS] = blank
                else:
                    dst[rows, PLANE:CELLS] = block[:, : CELLS - PLANE]
                    dst[rows, 0:PLANE] = blank


def turn(src, dst):
    def one(index, carry):
        at = pl.multiple_of(index * 128, 128)
        dst[:, pl.ds(at, 128)] = src[pl.ds(at, 128), :].T
        return carry

    lax.fori_loop(0, TALL // 128, one, 0)
    rest = TALL // 128 * 128
    dst[:, rest:TALL] = src[rest:TALL, :].T


def partial_sums(turned, columns, wide, dst, first, last):
    def one(index, carry):
        at = pl.multiple_of(index * PLANE, PLANE)
        total = jnp.dot(turned[...], columns[:, pl.ds(at, PLANE)], preferred_element_type=F32)
        total = total.reshape(2, 4, 2, RUN, PLANE)
        wide[:, :, :, :, pl.ds(at, PLANE)] = total
        dst[:, :, :, :, pl.ds(at, PLANE)] = total.astype(BF16)
        return carry

    lax.fori_loop(first, last, one, 0)


def conv_out(weights, gathered, wide, dst, sign):
    nine = 9 * OWN
    for d in range(PLANES):
        total = None
        for a in (-1, 0, 1):
            plane = d + sign * a
            if plane < 0 or plane >= PLANES:
                continue
            term = jnp.dot(
                weights[pl.ds((a + 1) * nine, nine), :],
                gathered[:, :, :, :, pl.ds(plane * PLANE, PLANE)].reshape(ALL, PLANE),
                preferred_element_type=F32,
            )
            total = term if total is None else total + term
        wide[:, pl.ds(d * PLANE, PLANE)] = total

    def one(index, carry):
        at = pl.multiple_of(index * 16, 16)
        total = jnp.zeros((16, CELLS), F32)
        for b in (-1, 0, 1):
            for c in (-1, 0, 1):
                tap = 3 * (b + 1) + c + 1
                total = total + moved(wide[pl.ds(tap * OWN + at, 16), :], sign * b, sign * c)
        dst[pl.ds(at, 16), :] = total.astype(BF16)
        return carry

    lax.fori_loop(0, OWN // 16, one, 0)


def kernel(
    volume_in, w_first_in, gain_in, w_second_in, cotangent_in,
    output_to, grad_volume_to, grad_first_to, grad_gain_to, grad_second_to,
    volume, w_first, w_second, cotangent, output, grad_volume, grad_first, grad_second,
    gain, grad_gain, vol_cols, cot_cols, turned, act, dpre,
    sums_a, wide_a, y_in_a, x_send_a, x_recv_a, x_in_a, y_send_a, y_recv_a, kept_a,
    sums_b, wide_b, y_in_b, x_send_b, x_recv_b, x_in_b, y_send_b, y_recv_b, kept_b,
    normed, sigma, inverse, wide,
    product, core_out, core_in, z_out, z_in, keep, x_out, x_in,
    gain_all, gain_core, gain_z, gain_x, send_sems, recv_sems, own_sems,
):
    dp = lax.axis_index("dp")
    chan = lax.axis_index("chan")
    x_lo, z, core = dp // 8, dp // 2 % 4, dp % 2
    y, x_hi = chan // 2, chan % 2
    pending = []
    moves = []

    def move(src, dst):
        copy = pltpu.make_async_copy(src, dst, own_sems.at[len(moves)])
        copy.start()
        moves.append(copy)
        return copy

    load_volume = move(volume_in, volume)
    load_first = move(w_first_in, w_first)
    load_cotangent = move(cotangent_in, cotangent)
    load_second = move(w_second_in, w_second)
    load_gain = move(gain_in, gain)

    def send(src, dst, device):
        index = len(pending)
        copy = pltpu.make_async_remote_copy(
            src_ref=src,
            dst_ref=dst,
            send_sem=send_sems.at[index],
            recv_sem=recv_sems.at[index],
            device_id=device,
            device_id_type=MESH,
        )
        copy.start()
        pending.append(copy)
        return copy

    peers = []
    for k in (4, 2, 6, 1, 5, 3, 7):
        other = (y + k // 2) % 4 * 2 + (x_hi + k % 2) % 2
        peers.append((other, (dp, other)))
    core_peer = (x_lo * 8 + z * 2 + 1 - core, chan)
    chan_x = (dp, y * 2 + 1 - x_hi)
    chan_y = {j: (dp, (y + j) % 4 * 2 + x_hi) for j in (1, 2, 3)}
    x_peer = ((1 - x_lo) * 8 + z * 2 + core, chan)
    z_peer = {j: (x_lo * 8 + (z + j) % 4 * 2 + core, chan) for j in (1, 2, 3)}

    barrier = pltpu.get_barrier_semaphore()
    everyone = [device for _, device in peers] + [core_peer, x_peer] + list(z_peer.values())
    for device in everyone:
        pl.semaphore_signal(barrier, inc=1, device_id=device, device_id_type=MESH)

    group_a = (sums_a, wide_a, y_in_a, x_send_a, x_recv_a, x_in_a, y_send_a, y_recv_a, kept_a)
    group_b = (sums_b, wide_b, y_in_b, x_send_b, x_recv_b, x_in_b, y_send_b, y_recv_b, kept_b)
    turns = (2, 1, 3)

    def scatter(group, half):
        sums, _, y_in, _, _, x_in, _, _, _ = group
        cells = pl.ds(half * (CELLS // 2), CELLS // 2)
        copies = [send(sums.at[1, :, 1 - x_hi, :, cells], x_in.at[:, :, cells], chan_x)]
        for j in turns:
            spot = sums.at[0, (y + j) % 4, :, :, cells]
            copies.append(send(spot, y_in.at[j - 1, :, :, cells], chan_y[j]))
        return copies

    def scatter_on(group, half, copies):
        _, wide, y_in, x_send, x_recv, x_in, y_send, y_recv, kept = group
        cells = pl.ds(half * (CELLS // 2), CELLS // 2)
        arrived(copies)

        def crossed(side):
            total = wide[0, y, side, :, cells]
            for slot in range(3):
                total = total + y_in[slot, side, :, cells].astype(F32)
            return total

        def along(j):
            row = (y + j) % 4
            return wide[1, row, x_hi, :, cells] + x_in[row, :, cells].astype(F32)

        x_send[:, cells] = crossed(1 - x_hi).astype(BF16)
        later = [send(x_send.at[:, cells], x_recv.at[:, cells], chan_x)]
        for j in turns:
            y_send[j - 1, :, cells] = along(j).astype(BF16)
            later.append(send(y_send.at[j - 1, :, cells], y_recv.at[j - 1, :, cells], chan_y[j]))
        kept[0, :, cells] = crossed(x_hi)
        kept[1, :, cells] = along(0)
        return later

    def share(block):
        own_first = block.at[0, y, x_hi]
        own_second = block.at[1, y, x_hi]
        across = send(own_second, own_second, chan_x)
        along = {j: send(own_first, own_first, chan_y[j]) for j in turns}
        return across, along, [send(own_first, own_first, chan_x)]

    def share_on(block, state):
        across, along, first = state
        across.wait_recv()
        pair = block.at[1, y]
        second = [send(pair, pair, chan_y[j]) for j in turns]
        for j in (1, 3, 2):
            along[j].wait_recv()
            spot = block.at[0, (y + 4 - j) % 4, x_hi]
            first.append(send(spot, spot, chan_x))
        return first, second

    def arrived(copies):
        for copy in copies:
            copy.wait_recv()

    load_volume.wait()
    build_columns(volume, vol_cols, 1)
    load_first.wait()
    turn(w_first, turned)
    partial_sums(turned, vol_cols, wide_a, sums_a, 0, 2)
    pl.semaphore_wait(barrier, len(everyone))
    first_low = scatter(group_a, 0)
    partial_sums(turned, vol_cols, wide_a, sums_a, 2, 4)
    first_high = scatter(group_a, 1)

    load_cotangent.wait()
    build_columns(cotangent, cot_cols, -1)
    load_second.wait()
    turn(w_second, turned)
    first_low = scatter_on(group_a, 0, first_low)
    partial_sums(turned, cot_cols, wide_b, sums_b, 0, 2)
    first_high = scatter_on(group_a, 1, first_high)
    second_low = scatter(group_b, 0)
    partial_sums(turned, cot_cols, wide_b, sums_b, 2, 4)

    load_gain.wait()
    own_row = lax.broadcasted_iota(jnp.int32, (OWN, ALL), 0)
    wanted = own_row // RUN * HALF + chan * RUN + own_row % RUN
    gain_own = jnp.sum(
        jnp.where(
            lax.broadcasted_iota(jnp.int32, (OWN, ALL), 1) == wanted,
            jnp.broadcast_to(gain[...], (OWN, ALL)),
            0.0,
        ),
        axis=1,
        keepdims=True,
    )
    scale = 1.0 / CELLS

    def summed(group, unit, at):
        _, _, _, _, x_recv, _, _, y_recv, kept = group
        rows = pl.ds(at, 16)
        total = kept[unit, rows, :]
        if unit == 0:
            return total + x_recv[rows, :].astype(F32)
        for slot in range(3):
            total = total + y_recv[slot, rows, :].astype(F32)
        return total

    arrived(first_low)
    arrived(first_high)
    for unit in range(2):
        for at in range(0, RUN, 16):
            line = unit * RUN + at
            gain_rows = gain_own[line : line + 16]
            pre = summed(group_a, unit, at)
            center = pre - jnp.sum(pre, axis=1, keepdims=True) * scale
            inv = lax.rsqrt(jnp.sum(center * center, axis=1, keepdims=True) * scale + NORM_EPS)
            unit_rows = center * inv
            scaled = gain_rows * unit_rows
            sig = jax.nn.sigmoid(scaled)
            normed[pl.ds(line, 16), :] = unit_rows
            sigma[pl.ds(line, 16), :] = sig
            inverse[pl.ds(line, 16), :] = jnp.broadcast_to(inv, (16, 128))
            act[unit, y, x_hi, pl.ds(at, 16), :] = (scaled * sig).astype(BF16)
    act_state = share(act)
    second_low = scatter_on(group_b, 0, second_low)
    second_high = scatter(group_b, 1)
    act_first, act_second = share_on(act, act_state)

    def z_rows(j):
        return pl.ds(pl.multiple_of((z + j) % 4 * ZBLOCK, ZBLOCK), ZBLOCK)

    def lanes(side):
        return pl.ds(pl.multiple_of(side * QUART, QUART), QUART)

    order = (2, 1, 3, 0)

    def reduce_start(columns, gathered, half, unit):
        crossing = {}
        for j in order:
            product[j] = lax.dot_general(
                columns[z_rows(j), :],
                gathered[half].reshape(HALF, CELLS),
                (((1,), (1,)), ((), ())),
                preferred_element_type=F32,
            )
            core_out[unit, j] = product[j, :, lanes(1 - core)].astype(BF16)
            crossing[j] = send(core_out.at[unit, j], core_in.at[unit, j], core_peer)
        z_copies = []
        for j in order:
            crossing[j].wait_recv()
            mine = product[j, :, lanes(core)] + core_in[unit, j].astype(F32)
            if j == 0:
                keep[unit] = mine
            else:
                z_out[unit, j - 1] = mine.astype(BF16)
                z_copies.append(send(z_out.at[unit, j - 1], z_in.at[unit, j - 1], z_peer[j]))
        return z_copies

    def reduce_x(z_copies, unit):
        arrived(z_copies)
        total = keep[unit]
        for slot in range(3):
            total = total + z_in[unit, slot].astype(F32)
        x_out[unit] = total.astype(BF16)
        return send(x_out.at[unit], x_in.at[unit], x_peer)

    factor = 1.0 / math.sqrt(lax.axis_size("dp") * CELLS)

    def spread_z(x_copy, unit, half, final):
        x_copy.wait_recv()
        mine = lanes(half * 2 + core)
        final[z_rows(0), mine] = (
            (x_out[unit].astype(F32) + x_in[unit].astype(F32)) * factor
        ).astype(BF16)
        spot = final.at[z_rows(0), mine]
        copies = {j: send(spot, spot, z_peer[j]) for j in (2, 1, 3)}
        return copies, [send(spot, spot, core_peer)]

    def spread_core(state, half, final):
        to_z, to_core = state
        for j in (1, 3, 2):
            to_z[j].wait_recv()
            spot = final.at[z_rows(4 - j), lanes(half * 2 + core)]
            to_core.append(send(spot, spot, core_peer))
        return to_core

    arrived(act_first)
    z_0 = reduce_start(cot_cols, act, 0, 0)
    second_high = scatter_on(group_b, 1, second_high)
    arrived(act_second)
    z_1 = reduce_start(cot_cols, act, 1, 1)

    arrived(second_low)
    arrived(second_high)
    gain_tile = jnp.zeros((8, 128), F32)
    for unit in range(2):
        for at in range(0, RUN, 16):
            line = unit * RUN + at
            gain_rows = gain_own[line : line + 16]
            dact = summed(group_b, unit, at)
            unit_rows = normed[pl.ds(line, 16), :]
            sig = sigma[pl.ds(line, 16), :]
            inv = inverse[pl.ds(line, 16), 0:1]
            scaled = gain_rows * unit_rows
            dscaled = dact * sig * (1.0 + scaled * (1.0 - sig))
            part = jnp.sum(dscaled * unit_rows, axis=1, keepdims=True)
            first = unit * HALF + chan * RUN + at
            spot = lax.broadcasted_iota(jnp.int32, (16, 128), 1)
            here = lax.broadcasted_iota(jnp.int32, (16, 128), 0) + first % 128
            row = jnp.sum(jnp.where(spot == here, part, 0.0), axis=0, keepdims=True)
            line_at = lax.broadcasted_iota(jnp.int32, (8, 128), 0)
            gain_tile = gain_tile + jnp.where(line_at == first // 128, row, 0.0)
            dnormed = dscaled * gain_rows
            mean_d = jnp.sum(dnormed, axis=1, keepdims=True) * scale
            mean_u = jnp.sum(dnormed * unit_rows, axis=1, keepdims=True) * scale
            back = (dnormed - mean_d - unit_rows * mean_u) * inv
            dpre[unit, y, x_hi, pl.ds(at, 16), :] = back.astype(BF16)
    dpre_state = share(dpre)
    x_0 = reduce_x(z_0, 0)
    dpre_first, dpre_second = share_on(dpre, dpre_state)
    x_1 = reduce_x(z_1, 1)
    gain_all[7] = gain_tile
    gain_copies = [
        send(gain_all.at[7], gain_all.at[slot], device) for slot, (_, device) in enumerate(peers)
    ]
    state_0 = spread_z(x_0, 0, 0, grad_second)
    conv_out(w_second, act, wide, output, 1)
    moves_out = [move(output, output_to)]
    state_1 = spread_z(x_1, 1, 1, grad_second)

    arrived(dpre_first)
    z_2 = reduce_start(vol_cols, dpre, 0, 2)
    last = spread_core(state_0, 0, grad_second)
    arrived(gain_copies)
    total = gain_all[0]
    for slot in range(1, 8):
        total = total + gain_all[slot]
    gain_core[0] = total
    gain_core_copy = send(gain_core.at[0], gain_core.at[1], core_peer)
    arrived(dpre_second)
    z_3 = reduce_start(vol_cols, dpre, 1, 3)
    gain_core_copy.wait_recv()
    gain_z[z] = gain_core[0] + gain_core[1]
    gain_copies = [send(gain_z.at[z], gain_z.at[z], z_peer[j]) for j in (1, 2, 3)]
    x_2 = reduce_x(z_2, 2)
    last += spread_core(state_1, 1, grad_second)
    state_2 = spread_z(x_2, 2, 0, grad_first)
    arrived(gain_copies)
    gain_x[0] = (gain_z[0] + gain_z[1]) + (gain_z[2] + gain_z[3])
    gain_x_copy = send(gain_x.at[0], gain_x.at[1], x_peer)
    x_3 = reduce_x(z_3, 3)
    state_3 = spread_z(x_3, 3, 1, grad_first)
    conv_out(w_first, dpre, wide, grad_volume, -1)
    moves_out.append(move(grad_volume, grad_volume_to))
    gain_x_copy.wait_recv()
    gain_x[2] = (gain_x[0] + gain_x[1]) * factor
    row = jnp.broadcast_to(gain_x[2, pl.ds(chan // 2, 1), :], (8, 128))
    grad_gain[...] = jnp.where(chan % 2 == 0, row, pltpu.roll(row, OWN, axis=1))
    moves_out.append(move(grad_gain, grad_gain_to))
    arrived(last)
    moves_out.append(move(grad_second, grad_second_to))
    final = spread_core(state_2, 0, grad_first)
    final += spread_core(state_3, 1, grad_first)
    for half in range(2):
        arrived(final[4 * half : 4 * half + 4])
        spot = pl.ds(half * HALF, HALF)
        moves_out.append(move(grad_first.at[:, spot], grad_first_to.at[:, spot]))
    for copy in moves_out:
        copy.wait()
    for copy in pending:
        copy.wait_send()


def widen(output, grad_volume, grad_first, grad_gain, grad_second, *results):
    results[0][...] = output[...]
    results[1][...] = grad_volume[...]
    results[2][...] = grad_first[...].astype(F32)
    results[3][...] = grad_gain[0:1, 0:OWN]
    results[4][...] = grad_second[...].astype(F32)


def shards(volume, w_first, gain, w_second, cotangent):
    free = pl.BlockSpec(memory_space=pl.ANY)
    shape = jax.ShapeDtypeStruct
    scattering = [
        pltpu.VMEM((2, 4, 2, RUN, CELLS), BF16),
        pltpu.VMEM((2, 4, 2, RUN, CELLS), F32),
        pltpu.VMEM((3, 2, RUN, CELLS), BF16),
        pltpu.VMEM((RUN, CELLS), BF16),
        pltpu.VMEM((RUN, CELLS), BF16),
        pltpu.VMEM((4, RUN, CELLS), BF16),
        pltpu.VMEM((3, RUN, CELLS), BF16),
        pltpu.VMEM((3, RUN, CELLS), BF16),
        pltpu.VMEM((2, RUN, CELLS), F32),
    ]
    partial = pl.pallas_call(
        kernel,
        name="conv_pair",
        out_shape=(
            shape((OWN, CELLS), BF16),
            shape((OWN, CELLS), BF16),
            shape((TALL, ALL), BF16),
            shape((8, 128), F32),
            shape((TALL, ALL), BF16),
        ),
        in_specs=[free] * 5,
        out_specs=[free] * 5,
        scratch_shapes=[
            pltpu.VMEM((OWN, CELLS), BF16),
            pltpu.VMEM((TALL, ALL), BF16),
            pltpu.VMEM((TALL, ALL), BF16),
            pltpu.VMEM((OWN, CELLS), BF16),
            pltpu.VMEM((OWN, CELLS), BF16),
            pltpu.VMEM((OWN, CELLS), BF16),
            pltpu.VMEM((TALL, ALL), BF16),
            pltpu.VMEM((TALL, ALL), BF16),
            pltpu.VMEM((1, ALL), F32),
            pltpu.VMEM((8, 128), F32),
            pltpu.VMEM((TALL, CELLS), BF16),
            pltpu.VMEM((TALL, CELLS), BF16),
            pltpu.VMEM((ALL, TALL), BF16),
            pltpu.VMEM((2, 4, 2, RUN, CELLS), BF16),
            pltpu.VMEM((2, 4, 2, RUN, CELLS), BF16),
        ]
        + scattering
        + scattering
        + [
            pltpu.VMEM((OWN, CELLS), F32),
            pltpu.VMEM((OWN, CELLS), F32),
            pltpu.VMEM((OWN, 128), F32),
            pltpu.VMEM((9 * OWN, CELLS), F32),
            pltpu.VMEM((4, ZBLOCK, HALF), F32),
            pltpu.VMEM((4, 4, ZBLOCK, QUART), BF16),
            pltpu.VMEM((4, 4, ZBLOCK, QUART), BF16),
            pltpu.VMEM((4, 3, ZBLOCK, QUART), BF16),
            pltpu.VMEM((4, 3, ZBLOCK, QUART), BF16),
            pltpu.VMEM((4, ZBLOCK, QUART), F32),
            pltpu.VMEM((4, ZBLOCK, QUART), BF16),
            pltpu.VMEM((4, ZBLOCK, QUART), BF16),
            pltpu.VMEM((8, 8, 128), F32),
            pltpu.VMEM((2, 8, 128), F32),
            pltpu.VMEM((4, 8, 128), F32),
            pltpu.VMEM((3, 8, 128), F32),
            pltpu.SemaphoreType.DMA((132,)),
            pltpu.SemaphoreType.DMA((132,)),
            pltpu.SemaphoreType.DMA((12,)),
        ],
        compiler_params=pltpu.CompilerParams(
            collective_id=0, has_side_effects=True, vmem_limit_bytes=60 << 20
        ),
    )(
        volume[0],
        w_first.reshape(TALL, ALL),
        gain.reshape(1, ALL),
        w_second.transpose(0, 2, 1).reshape(TALL, ALL),
        cotangent[0],
    )
    small = pl.BlockSpec((OWN // 4, CELLS), lambda i: (i, 0))
    large = pl.BlockSpec((ZBLOCK, ALL), lambda i: (i, 0))
    output, grad_volume, grad_first, grad_gain, grad_second = pl.pallas_call(
        widen,
        name="widen",
        grid=(4,),
        out_shape=(
            shape((OWN, CELLS), BF16),
            shape((OWN, CELLS), BF16),
            shape((TALL, ALL), F32),
            shape((1, OWN), F32),
            shape((TALL, ALL), F32),
        ),
        in_specs=[small, small, large, pl.BlockSpec((8, 128), lambda i: (0, 0)), large],
        out_specs=[small, small, large, pl.BlockSpec((1, OWN), lambda i: (0, 0)), large],
    )(*partial)
    return (
        output[None],
        grad_volume[None],
        grad_first.reshape(TAPS, OWN, ALL),
        grad_gain[0],
        grad_second.reshape(TAPS, OWN, ALL).transpose(0, 2, 1),
    )


def solution(mesh):
    placed = (
        P("dp", "chan", None),
        P(None, "chan", None),
        P(),
        P(None, None, "chan"),
        P("dp", "chan", None),
    )
    return jax.shard_map(
        shards,
        mesh=mesh,
        in_specs=placed,
        out_specs=(
            P("dp", "chan", None),
            P("dp", "chan", None),
            P(None, "chan", None),
            P("chan"),
            P(None, None, "chan"),
        ),
        check_vma=False,
    )
```

time: 109 us -> 93.8 us (0.86)
  Pallas kernels: 99.9 us -> 93 us
  other arithmetic: 6.16 us -> 0 us
  local copies, waits for them, and re-layouts: 2.51 us -> 0 us
    pallas_call x1, Pallas kernels: 99.9 us -> 87.5 us  [shards(): pl.pallas_call(kernel, name='conv_pair', out_shape=(shape((OWN, CELLS), B...]
    pallas_call x0 -> x1, Pallas kernels: none -> 5.47 us  [shards(): pl.pallas_call(widen, name='widen', grid=(4,), out_shape=(shape((OWN, CEL...]
    reshape x1 -> x0, other arithmetic: 3.88 us -> none  [shards(): grad_first.astype(F32).reshape(TAPS, OWN, ALL)]
    transpose x1 -> x0, other arithmetic: 2.28 us -> none  [shards(): grad_second.astype(F32).reshape(TAPS, OWN, ALL).transpose(0, 2, 1)]
    unnamed x8 -> x0, local copies, waits for them, and re-layouts: 1.32 us -> none
    squeeze x1 -> x0, local copies, waits for them, and re-layouts: 1.19 us -> none  [shards(): grad_gain[0, :OWN]]
where the time goes in v2:
time: 93.8 us; the launch traced here: 93.6 us
  Pallas kernels  93 us (99%)
    pallas_call x1, Pallas kernels, shards(): pl.pallas_call(kernel, name='conv_pair', out_shape=(shape((OWN, CELLS), B...  87.5 us
    pallas_call x1, Pallas kernels, shards(): pl.pallas_call(widen, name='widen', grid=(4,), out_shape=(shape((OWN, CEL...  5.47 us

profile of v2, /device:TPU:1, one launch (start us, length us, event | category | flops | bytes accessed | tf_op | source)
XLA Modules:
  0.0 93.6 jit_solution(3555393843707574014)
XLA Ops:
  0.6 87.5 %conv_pair.1 = (bf16[64,1024]{1,0:T(8,128)(2,1)}, bf16[64,1024]{1,0:T(8,128)(2,1)}, bf16[1728,512]{1,0:T(8,128)(2,1)}, f32[8,128]{1,0:T(8,128)}, bf16[1728,512]{1,0:T(8,128)(2,1)}) custom-call(bf16[64,1024]{1,0:T(8,128)(2,1)} %bitcast.16, bf16[1728,512]{1,0:T(8,128)(2,1)} %bitcast.14, f32[1,512]{1,0:T(1,128)} %bitcast.18, bf16[1728,512]{1,0:T(8,128)(2,1)} %bitcast.15, ...), custom_call_target="tpu_custom_call" | custom-call | tf_op jit(solution)/shard_map/conv_pair/pallas_call | solution.py:464
  88.2 5.5 %widen.1 = (bf16[64,1024]{1,0:T(8,128)(2,1)}, bf16[64,1024]{1,0:T(8,128)(2,1)}, f32[1728,512]{1,0:T(8,128)}, f32[1,64]{1,0:T(1,128)}, f32[1728,512]{1,0:T(8,128)}) custom-call(bf16[64,1024]{1,0:T(8,128)(2,1)} %get-tuple-element.15.output, bf16[64,1024]{1,0:T(8,128)(2,1)} %get-tuple-element.16.grad_volume, bf16[1728,512]{1,0:T(8,128)(2,1)} %get-tuple-element.17.grad_first, ...), custom_call_target="tpu_custom_call" | custom-call | tf_op jit(solution)/shard_map/widen/pallas_call | solution.py:528

commit v3 on v2

--- a/solution.py
+++ b/solution.py
@@ -113,9 +113,8 @@
 
 def kernel(
     volume_in, w_first_in, gain_in, w_second_in, cotangent_in,
-    output_to, grad_volume_to, grad_first_to, grad_gain_to, grad_second_to,
-    volume, w_first, w_second, cotangent, output, grad_volume, grad_first, grad_second,
-    gain, grad_gain, vol_cols, cot_cols, turned, act, dpre,
+    output, grad_volume, grad_first, grad_gain, grad_second,
+    volume, w_first, w_second, cotangent, gain, vol_cols, cot_cols, turned, act, dpre,
     sums_a, wide_a, y_in_a, x_send_a, x_recv_a, x_in_a, y_send_a, y_recv_a, kept_a,
     sums_b, wide_b, y_in_b, x_send_b, x_recv_b, x_in_b, y_send_b, y_recv_b, kept_b,
     normed, sigma, inverse, wide,
@@ -393,7 +392,6 @@
     ]
     state_0 = spread_z(x_0, 0, 0, grad_second)
     conv_out(w_second, act, wide, output, 1)
-    moves_out = [move(output, output_to)]
     state_1 = spread_z(x_1, 1, 1, grad_second)
 
     arrived(dpre_first)
@@ -419,36 +417,32 @@
     x_3 = reduce_x(z_3, 3)
     state_3 = spread_z(x_3, 3, 1, grad_first)
     conv_out(w_first, dpre, wide, grad_volume, -1)
-    moves_out.append(move(grad_volume, grad_volume_to))
     gain_x_copy.wait_recv()
     gain_x[2] = (gain_x[0] + gain_x[1]) * factor
     row = jnp.broadcast_to(gain_x[2, pl.ds(chan // 2, 1), :], (8, 128))
     grad_gain[...] = jnp.where(chan % 2 == 0, row, pltpu.roll(row, OWN, axis=1))
-    moves_out.append(move(grad_gain, grad_gain_to))
     arrived(last)
-    moves_out.append(move(grad_second, grad_second_to))
     final = spread_core(state_2, 0, grad_first)
     final += spread_core(state_3, 1, grad_first)
-    for half in range(2):
-        arrived(final[4 * half : 4 * half + 4])
-        spot = pl.ds(half * HALF, HALF)
-        moves_out.append(move(grad_first.at[:, spot], grad_first_to.at[:, spot]))
-    for copy in moves_out:
-        copy.wait()
+    arrived(final)
     for copy in pending:
         copy.wait_send()
 
 
 def widen(output, grad_volume, grad_first, grad_gain, grad_second, *results):
-    results[0][...] = output[...]
-    results[1][...] = grad_volume[...]
-    results[2][...] = grad_first[...].astype(F32)
+    step = pl.program_id(0)
+    few = pl.ds(pl.multiple_of(step * (OWN // 4), OWN // 4), OWN // 4)
+    many = pl.ds(pl.multiple_of(step * ZBLOCK, ZBLOCK), ZBLOCK)
+    results[0][...] = output[few, :]
+    results[1][...] = grad_volume[few, :]
+    results[2][...] = grad_first[many, :].astype(F32)
     results[3][...] = grad_gain[0:1, 0:OWN]
-    results[4][...] = grad_second[...].astype(F32)
+    results[4][...] = grad_second[many, :].astype(F32)
 
 
 def shards(volume, w_first, gain, w_second, cotangent):
     free = pl.BlockSpec(memory_space=pl.ANY)
+    vmem = pl.BlockSpec(memory_space=pltpu.VMEM)
     shape = jax.ShapeDtypeStruct
     scattering = [
         pltpu.VMEM((2, 4, 2, RUN, CELLS), BF16),
@@ -465,25 +459,20 @@
         kernel,
         name="conv_pair",
         out_shape=(
-            shape((OWN, CELLS), BF16),
-            shape((OWN, CELLS), BF16),
-            shape((TALL, ALL), BF16),
-            shape((8, 128), F32),
-            shape((TALL, ALL), BF16),
+            pltpu.VMEM((OWN, CELLS), BF16),
+            pltpu.VMEM((OWN, CELLS), BF16),
+            pltpu.VMEM((TALL, ALL), BF16),
+            pltpu.VMEM((8, 128), F32),
+            pltpu.VMEM((TALL, ALL), BF16),
         ),
         in_specs=[free] * 5,
-        out_specs=[free] * 5,
+        out_specs=[vmem] * 5,
         scratch_shapes=[
             pltpu.VMEM((OWN, CELLS), BF16),
             pltpu.VMEM((TALL, ALL), BF16),
             pltpu.VMEM((TALL, ALL), BF16),
             pltpu.VMEM((OWN, CELLS), BF16),
-            pltpu.VMEM((OWN, CELLS), BF16),
-            pltpu.VMEM((OWN, CELLS), BF16),
-            pltpu.VMEM((TALL, ALL), BF16),
-            pltpu.VMEM((TALL, ALL), BF16),
             pltpu.VMEM((1, ALL), F32),
-            pltpu.VMEM((8, 128), F32),
             pltpu.VMEM((TALL, CELLS), BF16),
             pltpu.VMEM((TALL, CELLS), BF16),
             pltpu.VMEM((ALL, TALL), BF16),
@@ -514,14 +503,19 @@
             pltpu.SemaphoreType.DMA((12,)),
         ],
         compiler_params=pltpu.CompilerParams(
-            collective_id=0, has_side_effects=True, vmem_limit_bytes=60 << 20
+            collective_id=0, has_side_effects=True, vmem_limit_bytes=50 << 20
         ),
     )(
-        volume[0],
-        w_first.reshape(TALL, ALL),
-        gain.reshape(1, ALL),
-        w_second.transpose(0, 2, 1).reshape(TALL, ALL),
-        cotangent[0],
+        *[
+            pltpu.with_memory_space_constraint(value, pltpu.HBM)
+            for value in (
+                volume[0],
+                w_first.reshape(TALL, ALL),
+                gain.reshape(1, ALL),
+                w_second.transpose(0, 2, 1).reshape(TALL, ALL),
+                cotangent[0],
+            )
+        ]
     )
     small = pl.BlockSpec((OWN // 4, CELLS), lambda i: (i, 0))
     large = pl.BlockSpec((ZBLOCK, ALL), lambda i: (i, 0))
@@ -529,6 +523,7 @@
         widen,
         name="widen",
         grid=(4,),
+        compiler_params=pltpu.CompilerParams(vmem_limit_bytes=16 << 20),
         out_shape=(
             shape((OWN, CELLS), BF16),
             shape((OWN, CELLS), BF16),
@@ -536,9 +531,9 @@
             shape((1, OWN), F32),
             shape((TALL, ALL), F32),
         ),
-        in_specs=[small, small, large, pl.BlockSpec((8, 128), lambda i: (0, 0)), large],
+        in_specs=[vmem] * 5,
         out_specs=[small, small, large, pl.BlockSpec((1, OWN), lambda i: (0, 0)), large],
-    )(*partial)
+    )(*[pltpu.with_memory_space_constraint(value, pltpu.VMEM) for value in partial])
     return (
         output[None],
         grad_volume[None],

time: 93.8 us -> 90.6 us (0.966)
  Pallas kernels: 93 us -> 89.8 us
    pallas_call x2, Pallas kernels: 93 us -> 89.8 us  [the longest x1 86.6 us: shards(): pl.pallas_call(kernel, name='conv_pair', out_shape=(pltpu.VMEM((OWN, CELL...]
where the time goes in v3:
time: 90.6 us; the launch traced here: 90.5 us
  Pallas kernels  89.8 us (99%)
    pallas_call x1, Pallas kernels, shards(): pl.pallas_call(kernel, name='conv_pair', out_shape=(pltpu.VMEM((OWN, CELL...  86.6 us
    pallas_call x1, Pallas kernels, shards(): pl.pallas_call(widen, name='widen', grid=(4,), compiler_params=pltpu.Comp...  3.22 us

profile of v3, /device:TPU:1, one launch (start us, length us, event | category | flops | bytes accessed | tf_op | source)
XLA Modules:
  0.0 90.5 jit_solution(16244594135842130268)
XLA Ops:
  0.6 86.6 %conv_pair.1 = (bf16[64,1024]{1,0:T(8,128)(2,1)S(1)}, bf16[64,1024]{1,0:T(8,128)(2,1)S(1)}, bf16[1728,512]{1,0:T(8,128)(2,1)S(1)}, f32[8,128]{1,0:T(8,128)S(1)}, bf16[1728,512]{1,0:T(8,128)(2,1)S(1)}) custom-call(bf16[64,1024]{1,0:T(8,128)(2,1)} %bitcast.16, bf16[1728,512]{1,0:T(8,128)(2,1)} %bitcast.14, f32[1,512]{1,0:T(1,128)} %bitcast.18, ...), custom_call_target="tpu_custom_call" | custom-call | tf_op jit(solution)/shard_map/conv_pair/pallas_call | solution.py:458
  87.2 3.2 %widen.1 = (bf16[64,1024]{1,0:T(8,128)(2,1)}, bf16[64,1024]{1,0:T(8,128)(2,1)}, f32[1728,512]{1,0:T(8,128)}, f32[1,64]{1,0:T(1,128)}, f32[1728,512]{1,0:T(8,128)}) custom-call(bf16[64,1024]{1,0:T(8,128)(2,1)S(1)} %get-tuple-element.15.output, bf16[64,1024]{1,0:T(8,128)(2,1)S(1)} %get-tuple-element.16.grad_volume, ...), custom_call_target="tpu_custom_call" | custom-call | tf_op jit(solution)/shard_map/widen/pallas_call | solution.py:522

commit v4 on v3

--- a/solution.py
+++ b/solution.py
@@ -299,7 +299,7 @@
     def lanes(side):
         return pl.ds(pl.multiple_of(side * QUART, QUART), QUART)
 
-    order = (2, 1, 3, 0)
+    order = (1, 3, 2, 0)
 
     def reduce_start(columns, gathered, half, unit):
         crossing = {}
@@ -351,9 +351,9 @@
             to_core.append(send(spot, spot, core_peer))
         return to_core
 
+    second_high = scatter_on(group_b, 1, second_high)
     arrived(act_first)
     z_0 = reduce_start(cot_cols, act, 0, 0)
-    second_high = scatter_on(group_b, 1, second_high)
     arrived(act_second)
     z_1 = reduce_start(cot_cols, act, 1, 1)
 

time: 90.6 us -> 89.9 us (level)
  no operation moved by 1% of the time
where the time goes in v4:
time: 89.9 us; the launch traced here: 89.8 us
  Pallas kernels  89.1 us (99%)
    pallas_call x1, Pallas kernels, shards(): pl.pallas_call(kernel, name='conv_pair', out_shape=(pltpu.VMEM((OWN, CELL...  85.9 us
    pallas_call x1, Pallas kernels, shards(): pl.pallas_call(widen, name='widen', grid=(4,), compiler_params=pltpu.Comp...  3.22 us

profile of v4, /device:TPU:1, one launch (start us, length us, event | category | flops | bytes accessed | tf_op | source)
XLA Modules:
  0.0 89.8 jit_solution(14802524309893987094)
XLA Ops:
  0.6 85.9 %conv_pair.1 = (bf16[64,1024]{1,0:T(8,128)(2,1)S(1)}, bf16[64,1024]{1,0:T(8,128)(2,1)S(1)}, bf16[1728,512]{1,0:T(8,128)(2,1)S(1)}, f32[8,128]{1,0:T(8,128)S(1)}, bf16[1728,512]{1,0:T(8,128)(2,1)S(1)}) custom-call(bf16[64,1024]{1,0:T(8,128)(2,1)} %bitcast.16, bf16[1728,512]{1,0:T(8,128)(2,1)} %bitcast.14, f32[1,512]{1,0:T(1,128)} %bitcast.18, ...), custom_call_target="tpu_custom_call" | custom-call | tf_op jit(solution)/shard_map/conv_pair/pallas_call | solution.py:458
  86.5 3.2 %widen.1 = (bf16[64,1024]{1,0:T(8,128)(2,1)}, bf16[64,1024]{1,0:T(8,128)(2,1)}, f32[1728,512]{1,0:T(8,128)}, f32[1,64]{1,0:T(1,128)}, f32[1728,512]{1,0:T(8,128)}) custom-call(bf16[64,1024]{1,0:T(8,128)(2,1)S(1)} %get-tuple-element.15.output, bf16[64,1024]{1,0:T(8,128)(2,1)S(1)} %get-tuple-element.16.grad_volume, ...), custom_call_target="tpu_custom_call" | custom-call | tf_op jit(solution)/shard_map/widen/pallas_call | solution.py:522

commit v5 on v4

--- a/solution.py
+++ b/solution.py
@@ -171,7 +171,7 @@
 
     group_a = (sums_a, wide_a, y_in_a, x_send_a, x_recv_a, x_in_a, y_send_a, y_recv_a, kept_a)
     group_b = (sums_b, wide_b, y_in_b, x_send_b, x_recv_b, x_in_b, y_send_b, y_recv_b, kept_b)
-    turns = (2, 1, 3)
+    turns = (1, 3, 2)
 
     def scatter(group, half):
         sums, _, y_in, _, _, x_in, _, _, _ = group

time: 89.9 us -> 89.2 us (level)
  no operation moved by 1% of the time
where the time goes in v5:
time: 89.2 us; the launch traced here: 89.1 us
  Pallas kernels  88.5 us (99%)
    pallas_call x1, Pallas kernels, shards(): pl.pallas_call(kernel, name='conv_pair', out_shape=(pltpu.VMEM((OWN, CELL...  85.2 us
    pallas_call x1, Pallas kernels, shards(): pl.pallas_call(widen, name='widen', grid=(4,), compiler_params=pltpu.Comp...  3.22 us

profile of v5, /device:TPU:1, one launch (start us, length us, event | category | flops | bytes accessed | tf_op | source)
XLA Modules:
  0.0 89.1 jit_solution(822663277292305230)
XLA Ops:
  0.6 85.2 %conv_pair.1 = (bf16[64,1024]{1,0:T(8,128)(2,1)S(1)}, bf16[64,1024]{1,0:T(8,128)(2,1)S(1)}, bf16[1728,512]{1,0:T(8,128)(2,1)S(1)}, f32[8,128]{1,0:T(8,128)S(1)}, bf16[1728,512]{1,0:T(8,128)(2,1)S(1)}) custom-call(bf16[64,1024]{1,0:T(8,128)(2,1)} %bitcast.16, bf16[1728,512]{1,0:T(8,128)(2,1)} %bitcast.14, f32[1,512]{1,0:T(1,128)} %bitcast.18, ...), custom_call_target="tpu_custom_call" | custom-call | tf_op jit(solution)/shard_map/conv_pair/pallas_call | solution.py:458
  85.9 3.2 %widen.1 = (bf16[64,1024]{1,0:T(8,128)(2,1)}, bf16[64,1024]{1,0:T(8,128)(2,1)}, f32[1728,512]{1,0:T(8,128)}, f32[1,64]{1,0:T(1,128)}, f32[1728,512]{1,0:T(8,128)}) custom-call(bf16[64,1024]{1,0:T(8,128)(2,1)S(1)} %get-tuple-element.15.output, bf16[64,1024]{1,0:T(8,128)(2,1)S(1)} %get-tuple-element.16.grad_volume, ...), custom_call_target="tpu_custom_call" | custom-call | tf_op jit(solution)/shard_map/widen/pallas_call | solution.py:522
